TPU v7x, 32 devices: a whole 2x2x4 slice. The times are simulated.
32 devices in a mesh: section: 8 (over z, x), sp: 4 (over y, core).
Axes of the slice: x: 2, y: 2, z: 4, core: 2. Of those that a mesh axis runs over, the one named last changes fastest.
Arguments:
- slots: bfloat16 [8, 64, 3072], P('section', 'sp'), may hold values from -6 to 6
- patch_of_slot: int32 [8], replicated, may hold values from 0 to 7, each once
- step_of_slot: int32 [8], replicated, may hold values from 0 to 26
- modulation: bfloat16 [8, 28, 3, 3072], P('section'), may hold values from -4 to 4
- w_qkv: bfloat16 [8, 3072, 3, 2048], P('section', None, None, 'sp'), may hold values from -0.109375 to 0.109375
- qk_scale: bfloat16 [8, 2, 128], P('section'), may hold values from 0.25 to 4
- w_mlp_in: bfloat16 [8, 3072, 6144], P('section', None, 'sp'), may hold values from -0.109375 to 0.109375
- w_attn_out: bfloat16 [8, 2048, 3072], P('section', 'sp'), may hold values from -0.125 to 0.125
- w_mlp_out: bfloat16 [8, 6144, 3072], P('section', 'sp'), may hold values from -0.078125 to 0.078125
- kv_cache: bfloat16 [8, 2, 512, 2048], P('section', None, None, 'sp'), may hold values from -130 to 130
Outputs:
- slots_out: bfloat16 [8, 64, 3072], P('section', 'sp')
- kv_cache_out: bfloat16 [8, 2, 512, 2048], P('section', None, None, 'sp')
Inputs may be any that keep to these rules, and one draw needn't show every extreme that they name: `patch_of_slot`: each patch id names exactly one slot.
All inputs are finite; a program needn't handle non-finite values.
Results may differ from a plain program's by a relative error of at most 0.012.
The roundings to bfloat16 on the way count: a program that leaves them out, or rounds other values in their place, can miss the bound.
Values may be sent and summed in bfloat16 or wider, within the bound.
A program may use at most 128 MiB of HBM per device.

v0:
```python
import math
import jax
import jax.numpy as jnp
from jax import lax
from jax.sharding import PartitionSpec as P

HD = 128
ROUNDS = 2


def shifted_2(x, axis, by):
    length = lax.axis_size(axis)
    return lax.ppermute(x, axis, [(i, (i + by) % length) for i in range(length)])


def slot_labels(patch_of_slot, step_of_slot, section_id, sections, round_id):
    anchor = section_id - round_id
    wrapped = (anchor < 0).astype(jnp.int32)
    anchor = anchor + wrapped * sections
    patch_id = lax.dynamic_index_in_dim(patch_of_slot, anchor, 0, keepdims=False)
    timestep = lax.dynamic_index_in_dim(step_of_slot, anchor, 0, keepdims=False) + wrapped
    return (patch_id, timestep)


def modulate(slot, table, timestep):
    factors = lax.dynamic_index_in_dim(table, timestep, 0, keepdims=False).astype(jnp.float32)
    wide = slot.astype(jnp.float32)
    center = wide - jnp.mean(wide, axis=-1, keepdims=True)
    spread = jnp.mean(center * center, axis=-1, keepdims=True)
    normed = (center * lax.rsqrt(spread + 1e-06) * (1.0 + factors[1]) + factors[0]).astype(
        jnp.bfloat16
    )
    return (normed, factors[2])


def head_norm(part, gain):
    rows = part.shape[0]
    wide = part.astype(jnp.float32).reshape(rows, -1, HD)
    power = jnp.mean(wide * wide, axis=-1, keepdims=True)
    normed = wide * lax.rsqrt(power + 1e-06) * gain.astype(jnp.float32)
    return normed.astype(jnp.bfloat16).reshape(rows, -1)


def mix(normed, patch_id, keys, values, qkv_weight, norm_gain, inner_weight):
    patch_rows = normed.shape[0]
    projected = jnp.einsum(
        "rd,dce->rce", normed, qkv_weight, preferred_element_type=jnp.float32
    ).astype(jnp.bfloat16)
    query_normed = head_norm(projected[:, 0], norm_gain[0])
    key_normed = head_norm(projected[:, 1], norm_gain[1])
    first_row = patch_id * patch_rows
    keys = lax.dynamic_update_slice_in_dim(keys, key_normed, first_row, 0)
    values = lax.dynamic_update_slice_in_dim(values, projected[:, 2], first_row, 0)
    local_heads = qkv_weight.shape[2] // HD
    queries = query_normed.reshape(patch_rows, local_heads, HD)
    key_heads = keys.reshape(keys.shape[0], local_heads, HD)
    value_heads = values.reshape(values.shape[0], local_heads, HD)
    scores = jnp.einsum(
        "rhd,thd->hrt", queries, key_heads, preferred_element_type=jnp.float32
    ) / math.sqrt(HD)
    shifted = jnp.exp(scores - jnp.max(scores, axis=-1, keepdims=True))
    weights = (shifted / jnp.sum(shifted, axis=-1, keepdims=True)).astype(jnp.bfloat16)
    attention = jnp.einsum(
        "hrt,thd->rhd", weights, value_heads, preferred_element_type=jnp.float32
    ).astype(jnp.bfloat16)
    attention = attention.reshape(patch_rows, local_heads * HD)
    activity = jax.nn.gelu(
        jnp.dot(normed, inner_weight, preferred_element_type=jnp.float32), approximate=True
    ).astype(jnp.bfloat16)
    return (attention, activity, keys, values)


def shards(
    slots,
    patch_of_slot,
    step_of_slot,
    modulation,
    w_qkv,
    qk_scale,
    w_mlp_in,
    w_attn_out,
    w_mlp_out,
    kv_cache,
):
    sections = lax.axis_size("section")
    section_id = lax.axis_index("section")
    table = modulation[0]
    qkv_weight = w_qkv[0]
    norm_gain = qk_scale[0]
    inner_weight = w_mlp_in[0]
    attention_weight = w_attn_out[0]
    outer_weight = w_mlp_out[0]
    keys = kv_cache[0, 0]
    values = kv_cache[0, 1]
    current = slots[0]
    for round_id in range(ROUNDS):
        patch_id, timestep = slot_labels(
            patch_of_slot, step_of_slot, section_id, sections, round_id
        )
        normed, gate = modulate(current, table, timestep)
        gathered = lax.all_gather(normed, "sp", axis=0, tiled=True)
        attention, activity, keys, values = mix(
            gathered, patch_id, keys, values, qkv_weight, norm_gain, inner_weight
        )
        summed = lax.psum_scatter(
            jnp.dot(attention, attention_weight, preferred_element_type=jnp.float32)
            + jnp.dot(activity, outer_weight, preferred_element_type=jnp.float32),
            "sp",
            scatter_dimension=0,
            tiled=True,
        )
        current = (current.astype(jnp.float32) + gate * summed).astype(jnp.bfloat16)
        current = shifted_2(current, "section", 1)
    return (current[None], jnp.stack([keys, values])[None])


def solution(mesh):
    return jax.shard_map(
        shards,
        mesh=mesh,
        in_specs=(
            P("section", "sp", None),
            P(),
            P(),
            P("section", None, None, None),
            P("section", None, None, "sp"),
            P("section", None, None),
            P("section", None, "sp"),
            P("section", "sp", None),
            P("section", "sp", None),
            P("section", None, None, "sp"),
        ),
        out_specs=(P("section", "sp", None), P("section", None, None, "sp")),
        check_vma=False,
    )
```

profile of v0, /device:TPU:0, one launch (start us, length us, event | category | flops | bytes accessed | tf_op | source)
XLA Modules:
  0.0 167.5 jit_solution(4243457292436387553)
XLA Ops:
  7.2 1.5 fusion.120
  10.0 1.1 dynamic-slice_convert_fusion
  11.1 1.0 convert_reduce_fusion.1
  12.1 1.1 fusion.78
  13.3 1.0 fusion.81
  14.3 8.0 %all_gather.6 = bf16[64,3072]{1,0:T(8,128)(2,1)S(1)} all-gather(bf16[16,3072]{1,0:T(8,128)(2,1)S(1)} %fusion.81), channel_id=1, replica_groups=mesh['section'=8,'sp'=4] {'sp'}, dimensions={0}, use_global_device_ids=true | all-gather | bytes 491520 | tf_op jit(solution)/shard_map/all_gather | solution.py:101
  22.2 0.7 copy-done.1
  23.0 5.4 %fusion.20 = bf16[64,3,512]{2,0,1:T(8,128)(2,1)S(1)} fusion(bf16[1,3072,3,512]{3,1,2,0:T(8,128)(2,1)} %param.14, bf16[64,3072]{1,0:T(8,128)(2,1)S(1)} %all_gather.6), kind=kOutput, calls=%fused_computation.24 | convolution fusion | flops 604078080 | bytes 10027008 | tf_op jit(solution)/shard_map/rd,dce->rce/dot_general | solution.py:46
  28.4 0.7 convert_multiply_fusion.1
  29.0 0.7 slice_convert_fusion.1
  29.7 0.9 mul.239
  30.6 0.8 reduce_sum.93
  31.4 0.8 add_rsqrt_fusion.2
  32.7 1.3 bitcast_convert_fusion.1
  34.6 2.3 %slice_bitcast_fusion = (bf16[512,512]{1,0:T(8,128)(2,1)}, bf16[512,512]{1,0:T(8,128)(2,1)}) fusion(bf16[1,2,512,512]{3,2,1,0:T(8,128)(2,1)} %param.19), kind=kLoop, calls=%fused_computation.43 | loop fusion | bytes 2097152 | tf_op jit(solution)/shard_map/squeeze | solution.py:93
  36.9 0.9 reshape.147
  38.6 0.9 multiply_convert_fusion.1
  39.6 1.3 fusion.99
  41.0 1.3 convolution_multiply_fusion.1
  42.3 0.8 copy-done.3
  43.3 2.0 %fusion.26 = bf16[4,8,8,128]{3,2,1,0:T(8,128)(2,1)S(1)} fusion(f32[4,64]{1,0:T(4,128)S(1)} %fusion.122, f32[4,64,512]{2,1,0:T(8,128)} %copy-done.3, bf16[512,512]{1,0:T(8,128)(2,1)} %get-tuple-element.9), kind=kOutput, calls=%fused_computation.28 | convolution fusion | flops 33981184 | bytes 1115136 | tf_op jit(solution)/shard_map/hrt,thd->rhd/dot_general | solution.py:63
  45.4 10.8 %fusion.4 = f32[64,3072]{1,0:T(8,128)} fusion(bf16[1,1536,3072]{2,1,0:T(8,128)(2,1)} %param.18, bf16[64,3072]{1,0:T(8,128)(2,1)} %copy-done.1, bf16[1,3072,1536]{2,1,0:T(8,128)(2,1)} %param.16), kind=kOutput, calls=%fused_computation.4 | convolution fusion | flops 1208844288 | bytes 20054016 | tf_op jit(solution)/shard_map/dot_general | solution.py:107
  56.2 2.7 %convolution_add_fusion.1 = f32[64,3072]{1,0:T(8,128)} fusion(f32[64,3072]{1,0:T(8,128)} %fusion.4, bf16[1,512,3072]{2,1,0:T(8,128)(2,1)S(1)} %copy-done, bf16[4,8,8,128]{3,2,1,0:T(8,128)(2,1)S(1)} %fusion.26), kind=kOutput, calls=%fused_computation.15 | convolution fusion | flops 201523200 | bytes 4784128 | tf_op jit(solution)/shard_map/dot_general | solution.py:106
  58.9 24.2 %reduce-scatter.3.cloned.1.call-done = f32[16,3072]{1,0:T(8,128)} async-done(((f32[64,3072]{1,0:T(8,128)}), f32[16,3072]{1,0:T(8,128)}) %reduce-scatter.3.cloned.1.call-update) | async-done | bytes 196624 | tf_op jit(solution)/shard_map/reduce_scatter | solution.py:105
  83.2 1.0 fusion.82
  84.1 1.5 collective-permute-start
  86.3 5.2 %collective-permute-done = bf16[16,3072]{1,0:T(8,128)(2,1)S(1)} collective-permute-done((bf16[16,3072]{1,0:T(8,128)(2,1)S(1)}, bf16[16,3072]{1,0:T(8,128)(2,1)S(1)}, u32[]{:S(2)}, u32[]{:S(2)}) %collective-permute-start) | collective-permute-done | bytes 98336 | tf_op jit(solution)/shard_map/ppermute | solution.py:13
  92.0 6.3 %all_gather.7 = bf16[64,3072]{1,0:T(8,128)(2,1)S(1)} all-gather(bf16[16,3072]{1,0:T(8,128)(2,1)S(1)} %fusion.77), channel_id=1, replica_groups=mesh['section'=8,'sp'=4] {'sp'}, dimensions={0}, use_global_device_ids=true | all-gather | bytes 491520 | tf_op jit(solution)/shard_map/all_gather | solution.py:101
  98.3 0.7 copy-done.2
  99.0 5.4 %fusion.23 = bf16[64,3,512]{2,0,1:T(8,128)(2,1)S(1)} fusion(bf16[1,3072,3,512]{3,1,2,0:T(8,128)(2,1)} %param.14, bf16[64,3072]{1,0:T(8,128)(2,1)S(1)} %all_gather.7), kind=kOutput, calls=%fused_computation.25 | convolution fusion | flops 604078080 | bytes 10027008 | tf_op jit(solution)/shard_map/rd,dce->rce/dot_general | solution.py:46
  104.4 0.7 convert_multiply_fusion
  105.1 0.7 slice_convert_fusion
  105.8 10.8 %fusion.2 = f32[64,3072]{1,0:T(8,128)} fusion(bf16[1,1536,3072]{2,1,0:T(8,128)(2,1)} %param.18, bf16[64,3072]{1,0:T(8,128)(2,1)} %copy-done.2, bf16[1,3072,1536]{2,1,0:T(8,128)(2,1)} %param.16), kind=kOutput, calls=%fused_computation.2 | convolution fusion | flops 1208844288 | bytes 20054016 | tf_op jit(solution)/shard_map/dot_general | solution.py:107
  116.5 1.6 mul.270
  118.1 1.0 reduce_sum.98
  119.2 1.6 reshape.151
  120.8 1.0 multiply_reduce_fusion
  121.9 1.0 multiply_convert_fusion
  123.0 0.7 fusion.98
  123.7 1.3 convolution_multiply_fusion
  125.1 0.8 copy-done.4
  126.1 1.9 %fusion.27 = bf16[4,8,8,128]{3,2,1,0:T(8,128)(2,1)S(1)} fusion(f32[4,64]{1,0:T(4,128)S(1)} %fusion.123, f32[4,64,512]{2,1,0:T(8,128)} %copy-done.4, bf16[512,512]{1,0:T(8,128)(2,1)} %get-tuple-element.7), kind=kOutput, calls=%fused_computation.29 | convolution fusion | flops 33981184 | bytes 1115136 | tf_op jit(solution)/shard_map/hrt,thd->rhd/dot_general | solution.py:63
  128.1 2.7 %convolution_add_fusion = f32[64,3072]{1,0:T(8,128)} fusion(f32[64,3072]{1,0:T(8,128)} %fusion.2, bf16[1,512,3072]{2,1,0:T(8,128)(2,1)S(1)} %copy-done, bf16[4,8,8,128]{3,2,1,0:T(8,128)(2,1)S(1)} %fusion.27), kind=kOutput, calls=%fused_computation.14 | convolution fusion | flops 201523200 | bytes 4784128 | tf_op jit(solution)/shard_map/dot_general | solution.py:106
  130.8 21.0 %reduce-scatter.5.cloned.1.call-done = f32[16,3072]{1,0:T(8,128)} async-done(((f32[64,3072]{1,0:T(8,128)}), f32[16,3072]{1,0:T(8,128)}) %reduce-scatter.5.cloned.1.call-update) | async-done | bytes 196624 | tf_op jit(solution)/shard_map/reduce_scatter | solution.py:105
  151.7 1.0 fusion.83
  152.7 1.5 collective-permute-start.1
  154.2 2.3 %maximum_bitcast_fusion = bf16[1,2,512,512]{3,2,1,0:T(8,128)(2,1)} fusion(bf16[1,512,512]{2,1,0:T(8,128)(2,1)} %bitcast.182, bf16[1,512,512]{2,1,0:T(8,128)(2,1)} %bitcast.181), kind=kLoop, calls=%fused_computation.30 | loop fusion | flops 524288 | bytes 2097152 | tf_op jit(solution)/shard_map/broadcast_in_dim | solution.py:114
  156.5 3.6 %collective-permute-done.1 = bf16[16,3072]{1,0:T(8,128)(2,1)S(1)} collective-permute-done((bf16[16,3072]{1,0:T(8,128)(2,1)S(1)}, bf16[16,3072]{1,0:T(8,128)(2,1)S(1)}, u32[]{:S(2)}, u32[]{:S(2)}) %collective-permute-start.1) | collective-permute-done | bytes 98336 | tf_op jit(solution)/shard_map/ppermute | solution.py:13
  (35 shorter events, 3.4 us)
Async XLA Ops:
  7.2 49.0 %copy-start = (bf16[1,512,3072]{2,1,0:T(8,128)(2,1)S(1)}, bf16[1,512,3072]{2,1,0:T(8,128)(2,1)}, u32[]{:S(2)}) copy-start(bf16[1,512,3072]{2,1,0:T(8,128)(2,1)} %param.17) | copy-start | bytes 9437188
  7.2 76.0 %reduce-scatter.3.cloned.1.call-start = ((), (), s32[]{:S(2)}) async-start(), calls=%async_computation.2 | async-start | bytes 983040 | tf_op jit(solution)/shard_map/reduce_scatter | solution.py:105
  22.2 0.7 copy-start.1
  42.3 0.8 copy-start.3
  45.4 37.8 %copy-start.5 = (bf16[1,16,3072]{2,1,0:T(8,128)(2,1)S(1)}, bf16[1,16,3072]{2,1,0:T(8,128)(2,1)}, u32[]{:S(2)}) copy-start(bf16[1,16,3072]{2,1,0:T(8,128)(2,1)} %param.10) | copy-start | bytes 294916
  58.9 92.9 %reduce-scatter.5.cloned.1.call-start = ((), (), s32[]{:S(2)}) async-start(), calls=%async_computation.3 | async-start | bytes 983040 | tf_op jit(solution)/shard_map/reduce_scatter | solution.py:105
  84.1 7.4 %collective-permute-start = (bf16[16,3072]{1,0:T(8,128)(2,1)S(1)}, bf16[16,3072]{1,0:T(8,128)(2,1)S(1)}, u32[]{:S(2)}, u32[]{:S(2)}) collective-permute-start(bf16[16,3072]{1,0:T(8,128)(2,1)S(1)} %fusion.82), channel_id=1, source_target_pairs={{0,4},{4,8},{8,12},{12,16},{16,20},{20,24},{24,28},{28,0},{1,5},{5... | collective-permute-start | bytes 294920 | tf_op jit(solution)/shard_map/ppermute | solution.py:13
  98.3 0.7 copy-start.2
  105.8 16.1 %copy-start.7 = (f32[128]{0:T(128)S(1)}, f32[128]{0:T(128)}, u32[]{:S(2)}) copy-start(f32[128]{0:T(128)} %get-tuple-element.20) | copy-start | bytes 1540
  105.8 17.3 %copy-start.6 = (f32[512]{0:T(512)S(1)}, f32[512]{0:T(512)}, u32[]{:S(2)}) copy-start(f32[512]{0:T(512)} %broadcast_bitcast_fusion) | copy-start | bytes 6148
  125.1 0.8 copy-start.4
  152.7 7.4 %collective-permute-start.1 = (bf16[16,3072]{1,0:T(8,128)(2,1)S(1)}, bf16[16,3072]{1,0:T(8,128)(2,1)S(1)}, u32[]{:S(2)}, u32[]{:S(2)}) collective-permute-start(bf16[16,3072]{1,0:T(8,128)(2,1)S(1)} %fusion.83), channel_id=1, source_target_pairs={{0,4},{4,8},{8,12},{12,16},{16,20},{20,24},{24,28},{28,0},{1,5},{5... | collective-permute-start | bytes 294920 | tf_op jit(solution)/shard_map/ppermute | solution.py:13
Sparse Core Ops, SparseCore 0:
  59.0 24.1 reduce-scatter.2
  130.9 20.7 reduce-scatter.4
where the time goes:
time: 169 us; the launch traced here: 168 us
  waiting for transfers between devices  54 us (32%)
  matrix products  44.3 us (26%)
  other arithmetic  21.6 us (13%)
  between operations  16.8 us (10%)
  blocking collectives  14.3 us (8%)
  local copies, waits for them, and re-layouts  13.4 us (8%)
  starting transfers between devices  3.15 us (2%)
    reduce_scatter x2, waiting for transfers between devices, shards(): lax.psum_scatter(jnp.dot(attention, attention_weight, preferred_element_t...  45.2 us
    dot_general x2, matrix products, shards(): jnp.dot(activity, outer_weight, preferred_element_type=jnp.float32)  21.6 us
    all_gather x2, blocking collectives, shards(): gathered = lax.all_gather(normed, 'sp', axis=0, tiled=True)  14.3 us
    dot_general x2, matrix products, mix(): jnp.einsum('rd,dce->rce', normed, qkv_weight, preferred_element_type=jnp....  10.8 us
    ppermute x2, waiting for transfers between devices, shifted_2(): lax.ppermute(x, axis, [(i, (i + by) % length) for i in range(length)])  8.74 us
    dot_general x2, matrix products, shards(): jnp.dot(attention, attention_weight, preferred_element_type=jnp.float32)  5.36 us
    dot_general x2, matrix products, mix(): jnp.einsum('hrt,thd->rhd', weights, value_heads, preferred_element_type=j...  3.95 us
    unnamed x17, local copies, waits for them, and re-layouts  3.75 us
  transfers between devices with their start and end apart: 4, of which 4 were waited for; matrix products, arithmetic and copies ran while one was open for 1% of the time, Pallas kernels for 0%

commit v1 on v0

--- a/solution.py
+++ b/solution.py
@@ -98,7 +98,18 @@
             patch_of_slot, step_of_slot, section_id, sections, round_id
         )
         normed, gate = modulate(current, table, timestep)
-        gathered = lax.all_gather(normed, "sp", axis=0, tiled=True)
+        later = lax.axis_index("sp")
+        right_arr = lax.axis_size("sp")
+        frame_out, current_block = (right_arr, later)
+        gathered, h_now = (normed, 1)
+        while h_now < frame_out:
+            res = lax.ppermute(
+                gathered, axis_name="sp", perm=[(u, u ^ h_now) for u in range(frame_out)]
+            )
+            x_next = jnp.concatenate([gathered, res], 0)
+            all_values = jnp.concatenate([res, gathered], 0)
+            gathered = jnp.where(current_block & h_now == 0, x_next, all_values)
+            h_now = 2 * h_now
         attention, activity, keys, values = mix(
             gathered, patch_id, keys, values, qkv_weight, norm_gain, inner_weight
         )

time: 169 us -> 179 us (1.059)
  blocking collectives: 14.3 us -> 0 us
  waiting for transfers between devices: 54 us -> 67.2 us
  other arithmetic: 21.6 us -> 25.5 us
  starting transfers between devices: 3.15 us -> 6.92 us
  local copies, waits for them, and re-layouts: 13.4 us -> 15.6 us
    all_gather x2 -> x0, blocking collectives: 14.3 us -> none  [shards(): gathered = lax.all_gather(normed, 'sp', axis=0, tiled=True)]
    ppermute x0 -> x4, waiting for transfers between devices: none -> 12.2 us  [shards(): lax.ppermute(gathered, axis_name='sp', perm=[(u, u ^ h_now) for u in rang...]
    ppermute x0 -> x4, starting transfers between devices: none -> 3.62 us  [shards(): lax.ppermute(gathered, axis_name='sp', perm=[(u, u ^ h_now) for u in rang...]
    reduce_sum x4, other arithmetic: 2.98 us -> 5.4 us  [head_norm(): power = jnp.mean(wide * wide, axis=-1, keepdims=True)]
  transfers between devices with their start and end apart: 4 -> 8, of which waited for: 4 -> 7; matrix products, arithmetic and copies ran while one was open for 1% -> 4% of each run, Pallas kernels for 0% -> 0%
where the time goes in v1:
time: 179 us; the launch traced here: 178 us
  waiting for transfers between devices  67.2 us (38%)
  matrix products  45.6 us (25%)
  other arithmetic  25.5 us (14%)
  between operations  16.9 us (9%)
  local copies, waits for them, and re-layouts  15.6 us (9%)
  starting transfers between devices  6.92 us (4%)
    reduce_scatter x2, waiting for transfers between devices, shards(): lax.psum_scatter(jnp.dot(attention, attention_weight, preferred_element_t...  45.5 us
    dot_general x2, matrix products, shards(): jnp.dot(activity, outer_weight, preferred_element_type=jnp.float32)  21.9 us
    ppermute x4, waiting for transfers between devices, shards(): lax.ppermute(gathered, axis_name='sp', perm=[(u, u ^ h_now) for u in rang...  12.2 us
    dot_general x2, matrix products, mix(): jnp.einsum('rd,dce->rce', normed, qkv_weight, preferred_element_type=jnp....  11 us
    ppermute x2, waiting for transfers between devices, shifted_2(): lax.ppermute(x, axis, [(i, (i + by) % length) for i in range(length)])  9.4 us
    reduce_sum x4, other arithmetic, head_norm(): power = jnp.mean(wide * wide, axis=-1, keepdims=True)  5.4 us
    dot_general x2, matrix products, shards(): jnp.dot(attention, attention_weight, preferred_element_type=jnp.float32)  5.39 us
    dot_general x2, matrix products, mix(): jnp.einsum('hrt,thd->rhd', weights, value_heads, preferred_element_type=j...  4.63 us
  transfers between devices with their start and end apart: 8, of which 7 were waited for; matrix products, arithmetic and copies ran while one was open for 4% of the time, Pallas kernels for 0%

profile of v1, /device:TPU:0, one launch (start us, length us, event | category | flops | bytes accessed | tf_op | source)
XLA Modules:
  0.0 177.6 jit_solution(1312130314269125636)
XLA Ops:
  7.2 1.5 fusion.126
  10.1 1.7 dynamic-slice_convert_fusion
  11.8 1.0 convert_reduce_fusion.1
  12.8 1.1 fusion.78
  13.9 1.0 fusion.81
  15.5 2.3 %slice_bitcast_fusion = (bf16[512,512]{1,0:T(8,128)(2,1)}, bf16[512,512]{1,0:T(8,128)(2,1)}) fusion(bf16[1,2,512,512]{3,2,1,0:T(8,128)(2,1)} %param.19), kind=kLoop, calls=%fused_computation.43 | loop fusion | bytes 2097152 | tf_op jit(solution)/shard_map/squeeze | solution.py:93
  17.8 1.2 bitcast_convert_fusion.1
  19.7 2.6 %collective-permute-start.1 = (bf16[32,3072]{1,0:T(8,128)(2,1)S(1)}, bf16[32,3072]{1,0:T(8,128)(2,1)S(1)}, u32[]{:S(2)}, u32[]{:S(2)}) collective-permute-start(bf16[32,3072]{1,0:T(8,128)(2,1)S(1)} %maximum_select_fusion.2), channel_id=1, source_target_pairs={{0,2},{1,3},{2,0},{3,1},{4,6},{5,7},{6,4},{7,5},{8,10},{9,11},{10,... | collective-permute-start | bytes 589832 | tf_op jit(solution)/shard_map/ppermute | solution.py:106
  23.0 4.9 %collective-permute-done.1 = bf16[32,3072]{1,0:T(8,128)(2,1)S(1)} collective-permute-done((bf16[32,3072]{1,0:T(8,128)(2,1)S(1)}, bf16[32,3072]{1,0:T(8,128)(2,1)S(1)}, u32[]{:S(2)}, u32[]{:S(2)}) %collective-permute-start.1) | collective-permute-done | bytes 196640 | tf_op jit(solution)/shard_map/ppermute | solution.py:106
  27.9 0.7 copy-done.6
  28.6 5.4 %fusion.20 = bf16[64,3,512]{2,0,1:T(8,128)(2,1)S(1)} fusion(bf16[1,3072,3,512]{3,1,2,0:T(8,128)(2,1)} %param.14, bf16[32,3072]{1,0:T(8,128)(2,1)S(1)} %collective-permute-done.1, bf16[32,3072]{1,0:T(8,128)(2,1)S(1)} %maximum_select_fusion.2, pred[]{:T(512)S(6)} %eq.8), kind=kOutput, calls=%fused_computation.24 | convolution fusion | flops 605847552 | bytes 10027009 | tf_op jit(solution)/shard_map/rd,dce->rce/dot_general | solution.py:46
  35.3 1.6 mul.239
  36.9 1.7 reduce_sum.93
  38.6 1.4 add_rsqrt_fusion.2
  39.9 1.6 reshape.147
  41.5 1.0 multiply_reduce_fusion.1
  42.6 1.0 multiply_convert_fusion.1
  43.6 0.9 mul.240
  45.2 1.3 convolution_multiply_fusion.1
  46.5 0.8 copy-done.1
  47.6 2.6 %fusion.26 = bf16[4,8,8,128]{3,2,1,0:T(8,128)(2,1)} fusion(f32[4,64]{1,0:T(4,128)S(1)} %fusion.128, f32[4,64,512]{2,1,0:T(8,128)} %copy-done.1, bf16[512,512]{1,0:T(8,128)(2,1)} %get-tuple-element.9), kind=kOutput, calls=%fused_computation.28 | convolution fusion | flops 33981184 | bytes 1115136 | tf_op jit(solution)/shard_map/hrt,thd->rhd/dot_general | solution.py:63
  50.2 10.9 %fusion.4 = f32[64,3072]{1,0:T(8,128)} fusion(bf16[1,1536,3072]{2,1,0:T(8,128)(2,1)} %param.18, bf16[1,3072,1536]{2,1,0:T(8,128)(2,1)} %param.16, bf16[32,3072]{1,0:T(8,128)(2,1)} %copy-done.6, bf16[32,3072]{1,0:T(8,128)(2,1)S(1)} %maximum_select_fusion.2, pred[]{:T(512)S(6)} %eq.8), kind=kOutput, calls=%fused_computation.4 | convolution fusion | flops 1210613760 | bytes 20054016 | tf_op jit(solution)/shard_map/dot_general | solution.py:118
  61.1 2.7 %convolution_add_fusion.1 = f32[64,3072]{1,0:T(8,128)} fusion(f32[64,3072]{1,0:T(8,128)} %fusion.4, bf16[1,512,3072]{2,1,0:T(8,128)(2,1)S(1)} %copy-done, bf16[4,8,8,128]{3,2,1,0:T(8,128)(2,1)} %fusion.26), kind=kOutput, calls=%fused_computation.15 | convolution fusion | flops 201523200 | bytes 4784128 | tf_op jit(solution)/shard_map/dot_general | solution.py:117
  63.9 24.8 %reduce-scatter.3.cloned.1.call-done = f32[16,3072]{1,0:T(8,128)} async-done(((f32[64,3072]{1,0:T(8,128)}), f32[16,3072]{1,0:T(8,128)}) %reduce-scatter.3.cloned.1.call-update) | async-done | bytes 196624 | tf_op jit(solution)/shard_map/reduce_scatter | solution.py:116
  88.7 1.0 fusion.82
  89.7 1.7 collective-permute-start.2
  91.4 5.8 %collective-permute-done.2 = bf16[16,3072]{1,0:T(8,128)(2,1)S(1)} collective-permute-done((bf16[16,3072]{1,0:T(8,128)(2,1)S(1)}, bf16[16,3072]{1,0:T(8,128)(2,1)S(1)}, u32[]{:S(2)}, u32[]{:S(2)}) %collective-permute-start.2) | collective-permute-done | bytes 98336 | tf_op jit(solution)/shard_map/ppermute | solution.py:13
  97.8 1.2 collective-permute-done.3
  100.1 6.1 %collective-permute-done.4 = bf16[32,3072]{1,0:T(8,128)(2,1)} collective-permute-done((bf16[32,3072]{1,0:T(8,128)(2,1)S(1)}, bf16[32,3072]{1,0:T(8,128)(2,1)}, u32[]{:S(2)}, u32[]{:S(2)}) %collective-permute-start.4) | collective-permute-done | bytes 196640 | tf_op jit(solution)/shard_map/ppermute | solution.py:106
  106.2 5.6 %fusion.23 = bf16[64,3,512]{2,0,1:T(8,128)(2,1)S(1)} fusion(bf16[1,3072,3,512]{3,1,2,0:T(8,128)(2,1)} %param.14, bf16[32,3072]{1,0:T(8,128)(2,1)} %collective-permute-done.4, bf16[32,3072]{1,0:T(8,128)(2,1)S(1)} %maximum_select_fusion.3, pred[]{:T(512)S(6)} %eq.8), kind=kOutput, calls=%fused_computation.25 | convolution fusion | flops 605847552 | bytes 10027009 | tf_op jit(solution)/shard_map/rd,dce->rce/dot_general | solution.py:46
  113.2 1.6 mul.270
  114.8 1.6 reduce_sum.98
  116.4 1.4 add_rsqrt_fusion
  117.8 1.6 reshape.151
  119.4 1.0 multiply_reduce_fusion
  120.5 1.0 multiply_convert_fusion
  121.5 0.9 mul.271
  122.4 0.7 fusion.98
  123.1 1.3 convolution_multiply_fusion
  124.4 0.8 copy-done.2
  125.4 2.0 %fusion.27 = bf16[4,8,8,128]{3,2,1,0:T(8,128)(2,1)S(1)} fusion(f32[4,64]{1,0:T(4,128)S(1)} %fusion.129, f32[4,64,512]{2,1,0:T(8,128)} %copy-done.2, bf16[512,512]{1,0:T(8,128)(2,1)} %get-tuple-element.7), kind=kOutput, calls=%fused_computation.29 | convolution fusion | flops 33981184 | bytes 1115136 | tf_op jit(solution)/shard_map/hrt,thd->rhd/dot_general | solution.py:63
  127.5 10.9 %fusion.2 = f32[64,3072]{1,0:T(8,128)} fusion(bf16[1,1536,3072]{2,1,0:T(8,128)(2,1)} %param.18, bf16[1,3072,1536]{2,1,0:T(8,128)(2,1)} %param.16, bf16[32,3072]{1,0:T(8,128)(2,1)} %collective-permute-done.4, bf16[32,3072]{1,0:T(8,128)(2,1)S(1)} %maximum_select_fusion.3, pred[]{:T(512)S(6)} %eq.8), kind=kOutput, calls=%fused_computation.2 | convolution fusion | flops 1210613760 | bytes 20054016 | tf_op jit(solution)/shard_map/dot_general | solution.py:118
  138.4 2.7 %convolution_add_fusion = f32[64,3072]{1,0:T(8,128)} fusion(f32[64,3072]{1,0:T(8,128)} %fusion.2, bf16[1,512,3072]{2,1,0:T(8,128)(2,1)S(1)} %copy-done, bf16[4,8,8,128]{3,2,1,0:T(8,128)(2,1)S(1)} %fusion.27), kind=kOutput, calls=%fused_computation.14 | convolution fusion | flops 201523200 | bytes 4784128 | tf_op jit(solution)/shard_map/dot_general | solution.py:117
  141.1 20.7 %reduce-scatter.5.cloned.1.call-done = f32[16,3072]{1,0:T(8,128)} async-done(((f32[64,3072]{1,0:T(8,128)}), f32[16,3072]{1,0:T(8,128)}) %reduce-scatter.5.cloned.1.call-update) | async-done | bytes 196624 | tf_op jit(solution)/shard_map/reduce_scatter | solution.py:116
  161.8 1.0 fusion.83
  162.8 1.5 collective-permute-start.5
  164.3 2.3 %maximum_bitcast_fusion = bf16[1,2,512,512]{3,2,1,0:T(8,128)(2,1)} fusion(bf16[1,512,512]{2,1,0:T(8,128)(2,1)} %bitcast.180, bf16[1,512,512]{2,1,0:T(8,128)(2,1)} %bitcast.179), kind=kLoop, calls=%fused_computation.30 | loop fusion | flops 524288 | bytes 2097152 | tf_op jit(solution)/shard_map/broadcast_in_dim | solution.py:125
  166.5 3.6 %collective-permute-done.5 = bf16[16,3072]{1,0:T(8,128)(2,1)S(1)} collective-permute-done((bf16[16,3072]{1,0:T(8,128)(2,1)S(1)}, bf16[16,3072]{1,0:T(8,128)(2,1)S(1)}, u32[]{:S(2)}, u32[]{:S(2)}) %collective-permute-start.5) | collective-permute-done | bytes 98336 | tf_op jit(solution)/shard_map/ppermute | solution.py:13
  (43 shorter events, 7.0 us)
Async XLA Ops:
  7.2 54.0 %copy-start = (bf16[1,512,3072]{2,1,0:T(8,128)(2,1)S(1)}, bf16[1,512,3072]{2,1,0:T(8,128)(2,1)}, u32[]{:S(2)}) copy-start(bf16[1,512,3072]{2,1,0:T(8,128)(2,1)} %param.17) | copy-start | bytes 9437188
  7.2 81.5 %reduce-scatter.3.cloned.1.call-start = ((), (), s32[]{:S(2)}) async-start(), calls=%async_computation.2 | async-start | bytes 983040 | tf_op jit(solution)/shard_map/reduce_scatter | solution.py:116
  15.0 4.7 %collective-permute-start = (bf16[16,3072]{1,0:T(8,128)(2,1)S(1)}, bf16[16,3072]{1,0:T(8,128)(2,1)S(1)}, u32[]{:S(2)}, u32[]{:S(2)}) collective-permute-start(bf16[16,3072]{1,0:T(8,128)(2,1)S(1)} %fusion.81), channel_id=1, source_target_pairs={{0,1},{1,0},{2,3},{3,2},{4,5},{5,4},{6,7},{7,6},{8,9},{9,8},{10,11... | collective-permute-start | bytes 294920 | tf_op jit(solution)/shard_map/ppermute | solution.py:106
  19.7 8.1 %collective-permute-start.1 = (bf16[32,3072]{1,0:T(8,128)(2,1)S(1)}, bf16[32,3072]{1,0:T(8,128)(2,1)S(1)}, u32[]{:S(2)}, u32[]{:S(2)}) collective-permute-start(bf16[32,3072]{1,0:T(8,128)(2,1)S(1)} %maximum_select_fusion.2), channel_id=1, source_target_pairs={{0,2},{1,3},{2,0},{3,1},{4,6},{5,7},{6,4},{7,5},{8,10},{9,11},{10,... | collective-permute-start | bytes 589832 | tf_op jit(solution)/shard_map/ppermute | solution.py:106
  27.9 0.7 copy-start.6
  46.5 0.8 copy-start.1
  50.2 38.5 %copy-start.3 = (bf16[1,16,3072]{2,1,0:T(8,128)(2,1)S(1)}, bf16[1,16,3072]{2,1,0:T(8,128)(2,1)}, u32[]{:S(2)}) copy-start(bf16[1,16,3072]{2,1,0:T(8,128)(2,1)} %param.10) | copy-start | bytes 294916
  50.2 41.2 %copy-start.7 = (f32[1,1,3,3072]{3,1,2,0:T(1,128)S(1)}, f32[1,1,3,3072]{3,1,2,0:T(1,128)}, u32[]{:S(2)}) copy-start(f32[1,1,3,3072]{3,1,2,0:T(1,128)} %get-tuple-element.4) | copy-start | bytes 110596
  63.9 97.9 %reduce-scatter.5.cloned.1.call-start = ((), (), s32[]{:S(2)}) async-start(), calls=%async_computation.3 | async-start | bytes 983040 | tf_op jit(solution)/shard_map/reduce_scatter | solution.py:116
  89.7 7.5 %collective-permute-start.2 = (bf16[16,3072]{1,0:T(8,128)(2,1)S(1)}, bf16[16,3072]{1,0:T(8,128)(2,1)S(1)}, u32[]{:S(2)}, u32[]{:S(2)}) collective-permute-start(bf16[16,3072]{1,0:T(8,128)(2,1)S(1)} %fusion.82), channel_id=1, source_target_pairs={{0,4},{4,8},{8,12},{12,16},{16,20},{20,24},{24,28},{28,0},{1,5},{5... | collective-permute-start | bytes 294920 | tf_op jit(solution)/shard_map/ppermute | solution.py:13
  97.2 0.6 copy-start.4
  97.7 1.4 collective-permute-start.3
  99.1 7.1 %collective-permute-start.4 = (bf16[32,3072]{1,0:T(8,128)(2,1)S(1)}, bf16[32,3072]{1,0:T(8,128)(2,1)}, u32[]{:S(2)}, u32[]{:S(2)}) collective-permute-start(bf16[32,3072]{1,0:T(8,128)(2,1)S(1)} %maximum_select_fusion.3), channel_id=1, source_target_pairs={{0,2},{1,3},{2,0},{3,1},{4,6},{5,7},{6,4},{7,5},{8,10},{9,11},{10,... | collective-permute-start | bytes 589832 | tf_op jit(solution)/shard_map/ppermute | solution.py:106
  124.4 0.8 copy-start.2
  127.5 34.4 %copy-start.5 = (bf16[16,3072]{1,0:T(8,128)(2,1)S(1)}, bf16[16,3072]{1,0:T(8,128)(2,1)}, u32[]{:S(2)}) copy-start(bf16[16,3072]{1,0:T(8,128)(2,1)} %copy-done.4) | copy-start | bytes 294916
  162.8 7.4 %collective-permute-start.5 = (bf16[16,3072]{1,0:T(8,128)(2,1)S(1)}, bf16[16,3072]{1,0:T(8,128)(2,1)S(1)}, u32[]{:S(2)}, u32[]{:S(2)}) collective-permute-start(bf16[16,3072]{1,0:T(8,128)(2,1)S(1)} %fusion.83), channel_id=1, source_target_pairs={{0,4},{4,8},{8,12},{12,16},{16,20},{20,24},{24,28},{28,0},{1,5},{5... | collective-permute-start | bytes 294920 | tf_op jit(solution)/shard_map/ppermute | solution.py:13
Sparse Core Ops, SparseCore 0:
  64.0 24.6 reduce-scatter.2
  141.2 20.5 reduce-scatter.4
